TPU v7x, 512 devices: a whole 4x4x16 slice. The times are simulated.
512 devices in a mesh: leaf: 128 (over y, z, core), panel: 4 (over x).
Axes of the slice: x: 4, y: 4, z: 16, core: 2. Of those that a mesh axis runs over, the one named last changes fastest.
Arguments:
- border: bfloat16 [128, 128, 8192], P('leaf', 'panel'), may hold values from -0.046875 to 0.046875
- solution: bfloat16 [128, 128, 128], P('leaf', 'panel'), may hold values from -6 to 6
- winv_top: bfloat16 [4096, 4096], P(None, ('leaf', 'panel')), as said below
- winv_mid: bfloat16 [4096, 8192], P(None, ('leaf', 'panel')), as said below
- coupling: bfloat16 [8192, 4096], P(('leaf', 'panel')), may hold values from -0.0625 to 0.0625
Outputs:
- top_adjoint: float32 [4096, 128], P(('leaf', 'panel'))
- mid_adjoint: float32 [8192, 128], P(('leaf', 'panel'))
Inputs may be any that keep to these rules, and one draw needn't show every extreme that they name: `winv_top`: each 4096 x 4096 block of the factor is lower triangular with a positive diagonal. `winv_mid`: each 4096 x 4096 block of the factor is lower triangular with a positive diagonal.
All inputs are finite; a program needn't handle non-finite values.
Results may differ from a plain program's by a relative error of at most 0.0003.
Values sent between devices are 32-bit elements; how exact they have to be, the bound alone decides.
A program may use at most 64 MiB of HBM per device.

v0:
```python
import jax
import jax.numpy as jnp
from jax import lax
from jax.sharding import PartitionSpec as P


def from_partner(value, axis, stride):
    mask = 2**stride
    pairs = [(source, source ^ mask) for source in range(lax.axis_size(axis))]
    return lax.ppermute(value, axis, pairs)


def split_half(buffer, chosen):
    half_rows = buffer.shape[0] // 2
    kept_half = lax.dynamic_slice_in_dim(buffer, chosen * half_rows, half_rows, 0)
    sent_half = lax.dynamic_slice_in_dim(buffer, (1 - chosen) * half_rows, half_rows, 0)
    return (kept_half, sent_half)


def split_parity(buffer, chosen):
    paired = buffer.reshape(buffer.shape[0] // 2, 2, buffer.shape[1])
    even_rows = paired[:, 0]
    odd_rows = paired[:, 1]
    kept_rows = jnp.where(chosen == 0, even_rows, odd_rows)
    sent_rows = jnp.where(chosen == 0, odd_rows, even_rows)
    return (kept_rows, sent_rows)


def partner_halving(top_part, mid_part, leaf_id, leaf_bits):
    for bit_pos in reversed(range(leaf_bits)):
        chosen = leaf_id >> bit_pos & 1
        outgoing = []
        top_part, sent_top = split_half(top_part, chosen)
        outgoing.append(sent_top)
        if bit_pos < leaf_bits - 1:
            mid_part, sent_mid = split_half(mid_part, chosen)
            outgoing.append(sent_mid)
        received = from_partner(jnp.concatenate(outgoing, 0), "leaf", bit_pos)
        position = 0
        top_part = top_part + received[: top_part.shape[0]]
        position = top_part.shape[0]
        if bit_pos < leaf_bits - 1:
            mid_part = mid_part + received[position:]
    return (top_part, mid_part)


def body(border, solution, winv_top, winv_mid, coupling):
    leaves = lax.axis_size("leaf")
    leaf_bits = leaves.bit_length() - 1
    front_rows = winv_top.shape[0]
    leaf_id = lax.axis_index("leaf")
    contribution = lax.dot_general(
        border[0], solution[0], (((0,), (0,)), ((), ())), preferred_element_type=jnp.float32
    )
    top_part = contribution[:front_rows]
    mid_part = contribution[front_rows:]
    top_block, mid_block = partner_halving(top_part, mid_part, leaf_id, leaf_bits)
    top_block, mid_block = (
        lax.psum_scatter(top_block, "panel", scatter_dimension=0, tiled=True),
        lax.psum_scatter(mid_block, "panel", scatter_dimension=0, tiled=True),
    )
    top_factor = winv_top.astype(jnp.float32)
    top_inner = lax.psum(
        jnp.dot(top_factor, top_block, precision=lax.Precision.HIGHEST), ("leaf", "panel")
    )
    top_adjoint = jnp.dot(top_factor.T, top_inner, precision=lax.Precision.HIGHEST)
    top_whole = lax.all_gather(top_adjoint, ("leaf", "panel"), axis=0, tiled=True)
    couple = coupling.astype(jnp.float32)
    mid_rhs = mid_block - jnp.dot(couple, top_whole, precision=lax.Precision.HIGHEST)
    mid_factor = winv_mid.astype(jnp.float32)
    group_block = jnp.dot(mid_factor, mid_rhs, precision=lax.Precision.HIGHEST)
    for bit_pos in reversed(range(leaf_bits - 1)):
        chosen = leaf_id >> bit_pos & 1
        kept_rows, sent_rows = split_parity(group_block, chosen)
        group_block = kept_rows + from_partner(sent_rows, "leaf", bit_pos)
    group_block = lax.psum(group_block, "panel")
    for bit_pos in range(leaf_bits - 1):
        chosen = leaf_id >> bit_pos & 1
        received = from_partner(group_block, "leaf", bit_pos)
        even_rows = jnp.where(chosen == 0, group_block, received)
        odd_rows = jnp.where(chosen == 0, received, group_block)
        group_block = jnp.stack([even_rows, odd_rows], 1).reshape(
            2 * group_block.shape[0], group_block.shape[1]
        )
    mid_adjoint = jnp.dot(mid_factor.T, group_block, precision=lax.Precision.HIGHEST)
    return (top_adjoint, mid_adjoint)


def solution(mesh):
    placed = (
        P("leaf", "panel", None),
        P("leaf", "panel", None),
        P(None, ("leaf", "panel")),
        P(None, ("leaf", "panel")),
        P(("leaf", "panel"), None),
    )
    return jax.shard_map(
        body,
        mesh=mesh,
        in_specs=placed,
        out_specs=(P(("leaf", "panel"), None), P(("leaf", "panel"), None)),
        check_vma=False,
    )
```

profile of v0, /device:TPU:1, one launch (start us, length us, event | category | flops | bytes accessed | tf_op | source)
XLA Modules:
  0.0 1222.7 jit_solution(14282266658055465502)
XLA Ops:
  10.5 1.6 fusion.6
  12.1 2.3 constant_dynamic-slice_fusion.12
  14.4 5.6 collective-permute-start
  20.1 19.9 %collective-permute-done = f32[2048,128]{1,0:T(8,128)} collective-permute-done((f32[2048,128]{1,0:T(8,128)}, f32[2048,128]{1,0:T(8,128)}, u32[]{:S(2)}, u32[]{:S(2)}) %collective-permute-start) | collective-permute-done | bytes 1048608 | tf_op jit(solution)/shard_map/ppermute | solution.py:10
  42.9 6.2 collective-permute-start.1
  49.1 33.1 %collective-permute-done.1 = f32[3072,128]{1,0:T(8,128)} collective-permute-done((f32[3072,128]{1,0:T(8,128)}, f32[3072,128]{1,0:T(8,128)}, u32[]{:S(2)}, u32[]{:S(2)}) %collective-permute-start.1) | collective-permute-done | bytes 1572896 | tf_op jit(solution)/shard_map/ppermute | solution.py:10
  85.1 15.7 %collective-permute-start.2 = (f32[1536,128]{1,0:T(8,128)S(1)}, f32[1536,128]{1,0:T(8,128)S(1)}, u32[]{:S(2)}, u32[]{:S(2)}) collective-permute-start(f32[1536,128]{1,0:T(8,128)S(1)} %pad_maximum_fusion.3), channel_id=1, source_target_pairs={{0,64},{4,68},{8,72},{12,76},{16,80},{20,84},{24,88},{28,92},{32,9... | collective-permute-start | bytes 2359304 | tf_op jit(solution)/shard_map/ppermute | solution.py:10
  100.8 24.3 %collective-permute-done.2 = f32[1536,128]{1,0:T(8,128)S(1)} collective-permute-done((f32[1536,128]{1,0:T(8,128)S(1)}, f32[1536,128]{1,0:T(8,128)S(1)}, u32[]{:S(2)}, u32[]{:S(2)}) %collective-permute-start.2) | collective-permute-done | bytes 786464 | tf_op jit(solution)/shard_map/ppermute | solution.py:10
  126.4 38.8 %collective-permute-start.3 = (f32[768,128]{1,0:T(8,128)S(1)}, f32[768,128]{1,0:T(8,128)S(1)}, u32[]{:S(2)}, u32[]{:S(2)}) collective-permute-start(f32[768,128]{1,0:T(8,128)S(1)} %pad_maximum_fusion.5), channel_id=1, source_target_pairs={{0,32},{4,36},{8,40},{12,44},{16,48},{20,52},{24,56},{28,60},{32,0... | collective-permute-start | bytes 1179656 | tf_op jit(solution)/shard_map/ppermute | solution.py:10
  165.2 38.6 %collective-permute-done.3 = f32[768,128]{1,0:T(8,128)S(1)} collective-permute-done((f32[768,128]{1,0:T(8,128)S(1)}, f32[768,128]{1,0:T(8,128)S(1)}, u32[]{:S(2)}, u32[]{:S(2)}) %collective-permute-start.3) | collective-permute-done | bytes 393248 | tf_op jit(solution)/shard_map/ppermute | solution.py:10
  203.9 1.9 collective-permute-start.4
  205.9 9.6 collective-permute-done.4
  215.6 1.9 collective-permute-start.5
  217.6 3.8 collective-permute-done.5
  221.5 3.3 collective-permute-start.6
  226.7 13.1 %all-reduce = f32[32,128]{1,0:T(8,128)S(1)} all-reduce(f32[32,128]{1,0:T(8,128)S(1)} %slice_add_fusion.11), channel_id=2, replica_groups=mesh['leaf'=128,'panel'=4] {'panel'}, use_global_device_ids=true, to_apply=%region_0.0.clone | all-reduce | flops 4096 | bytes 32768
  239.8 2.4 convolution_bitcast_fusion.1
  242.3 481.7 %all-reduce.3.cloned.1.call-done = f32[4096,128]{0,1:T(8,128)} async-done(((f32[4096,128]{0,1:T(8,128)}), f32[4096,128]{0,1:T(8,128)}) %all-reduce.3.cloned.1.call-update) | async-done | bytes 2097168 | tf_op jit(solution)/shard_map/psum | solution.py:63
  724.0 3.2 convolution_bitcast_fusion.4
  727.9 194.9 %all-gather.2.cloned.1.call-done = f32[4096,128]{1,0:T(8,128)} async-done(((f32[8,128]{1,0:T(8,128)}), f32[4096,128]{1,0:T(8,128)}) %all-gather.2.cloned.1.call-update) | async-done | bytes 2097168 | tf_op jit(solution)/shard_map/all_gather | solution.py:67
  922.8 2.4 convolution_bitcast_fusion.3
  925.2 3.1 convolution_bitcast_fusion
  928.3 1.9 copy.66
  930.2 2.5 broadcast_select_fusion
  932.8 3.2 collective-permute-start.7
  936.0 23.3 %collective-permute-done.7 = f32[2048,128]{1,0:T(8,128)S(1)} collective-permute-done((f32[2048,128]{1,0:T(8,128)}, f32[2048,128]{1,0:T(8,128)S(1)}, u32[]{:S(2)}, u32[]{:S(2)}) %collective-permute-start.7) | collective-permute-done | bytes 1048608 | tf_op jit(solution)/shard_map/ppermute | solution.py:10
  961.4 7.0 collective-permute-start.8
  968.4 39.4 %collective-permute-done.8 = f32[1024,128]{1,0:T(8,128)S(1)} collective-permute-done((f32[1024,128]{1,0:T(8,128)S(1)}, f32[1024,128]{1,0:T(8,128)S(1)}, u32[]{:S(2)}, u32[]{:S(2)}) %collective-permute-start.8) | collective-permute-done | bytes 524320 | tf_op jit(solution)/shard_map/ppermute | solution.py:10
  1008.3 1.9 collective-permute-start.9
  1010.2 16.4 %collective-permute-done.9 = f32[512,128]{1,0:T(8,128)S(1)} collective-permute-done((f32[512,128]{1,0:T(8,128)S(1)}, f32[512,128]{1,0:T(8,128)S(1)}, u32[]{:S(2)}, u32[]{:S(2)}) %collective-permute-start.9) | collective-permute-done | bytes 262176 | tf_op jit(solution)/shard_map/ppermute | solution.py:10
  1026.8 16.1 %collective-permute-start.10 = (f32[256,128]{1,0:T(8,128)S(1)}, f32[256,128]{1,0:T(8,128)S(1)}, u32[]{:S(2)}, u32[]{:S(2)}) collective-permute-start(f32[256,128]{1,0:T(8,128)S(1)} %bitcast.97), channel_id=1, source_target_pairs={{0,16},{4,20},{8,24},{12,28},{16,0},{20,4},{24,8},{28,12},{32,48},... | collective-permute-start | bytes 393224 | tf_op jit(solution)/shard_map/ppermute | solution.py:10
  1042.9 4.4 collective-permute-done.10
  1047.4 1.9 collective-permute-start.11
  1049.3 3.1 collective-permute-done.11
  1052.5 9.6 collective-permute-start.12
  1062.9 11.6 psum.15
  1074.4 6.0 collective-permute-start.13
  1081.4 2.7 collective-permute-start.14
  1084.1 2.3 collective-permute-done.14
  1086.5 1.9 collective-permute-start.15
  1088.5 8.5 collective-permute-done.15
  1097.3 3.8 collective-permute-start.16
  1101.1 24.7 %collective-permute-done.16 = f32[512,128]{1,0:T(8,128)S(1)} collective-permute-done((f32[512,128]{1,0:T(8,128)S(1)}, f32[512,128]{1,0:T(8,128)S(1)}, u32[]{:S(2)}, u32[]{:S(2)}) %collective-permute-start.16) | collective-permute-done | bytes 262176 | tf_op jit(solution)/shard_map/ppermute | solution.py:10
  1126.3 7.0 collective-permute-start.17
  1133.3 45.6 %collective-permute-done.17 = f32[1024,128]{1,0:T(8,128)S(1)} collective-permute-done((f32[1024,128]{1,0:T(8,128)S(1)}, f32[1024,128]{1,0:T(8,128)S(1)}, u32[]{:S(2)}, u32[]{:S(2)}) %collective-permute-start.17) | collective-permute-done | bytes 524320 | tf_op jit(solution)/shard_map/ppermute | solution.py:10
  1179.8 1.9 collective-permute-start.18
  1181.8 24.2 %collective-permute-done.18 = f32[2048,128]{1,0:T(8,128)S(1)} collective-permute-done((f32[2048,128]{1,0:T(8,128)S(1)}, f32[2048,128]{1,0:T(8,128)S(1)}, u32[]{:S(2)}, u32[]{:S(2)}) %collective-permute-start.18) | collective-permute-done | bytes 1048608 | tf_op jit(solution)/shard_map/ppermute | solution.py:10
  1206.3 7.6 copy.72
  (88 shorter events, 19.9 us)
Async XLA Ops:
  8.0 1.0 copy-start
  8.0 716.0 %all-reduce.3.cloned.1.call-start = ((), (), s32[]{:S(2)}) async-start(), calls=%async_computation.1 | async-start | bytes 4194304 | tf_op jit(solution)/shard_map/psum | solution.py:63
  14.4 25.6 %collective-permute-start = (f32[2048,128]{1,0:T(8,128)}, f32[2048,128]{1,0:T(8,128)}, u32[]{:S(2)}, u32[]{:S(2)}) collective-permute-start(f32[2048,128]{1,0:T(8,128)} %constant_dynamic-slice_fusion.12), channel_id=1, source_target_pairs={{0,256},{4,260},{8,264},{12,268},{16,272},{20,276},{24,280},{28,28... | collective-permute-start | bytes 3145736 | tf_op jit(solution)/shard_map/ppermute | solution.py:10
  20.0 20.0 %copy-start.1 = (f32[4096,128]{1,0:T(8,128)S(1)}, f32[4096,128]{1,0:T(8,128)}, u32[]{:S(2)}) copy-start(f32[4096,128]{1,0:T(8,128)} %get-tuple-element.2) | copy-start | bytes 6291460
  41.4 1.5 copy-start.2
  42.9 39.3 %collective-permute-start.1 = (f32[3072,128]{1,0:T(8,128)}, f32[3072,128]{1,0:T(8,128)}, u32[]{:S(2)}, u32[]{:S(2)}) collective-permute-start(f32[3072,128]{1,0:T(8,128)} %pad_maximum_fusion.1), channel_id=1, source_target_pairs={{0,128},{4,132},{8,136},{12,140},{16,144},{20,148},{24,152},{28,15... | collective-permute-start | bytes 4718600 | tf_op jit(solution)/shard_map/ppermute | solution.py:10
  49.0 34.5 %copy-start.3 = (f32[2048,128]{1,0:T(8,128)S(1)}, f32[2048,128]{1,0:T(8,128)}, u32[]{:S(2)}) copy-start(f32[2048,128]{1,0:T(8,128)} %copy-done.2) | copy-start | bytes 3145732
  83.5 1.6 copy-start.4
  85.1 40.0 %collective-permute-start.2 = (f32[1536,128]{1,0:T(8,128)S(1)}, f32[1536,128]{1,0:T(8,128)S(1)}, u32[]{:S(2)}, u32[]{:S(2)}) collective-permute-start(f32[1536,128]{1,0:T(8,128)S(1)} %pad_maximum_fusion.3), channel_id=1, source_target_pairs={{0,64},{4,68},{8,72},{12,76},{16,80},{20,84},{24,88},{28,92},{32,9... | collective-permute-start | bytes 2359304 | tf_op jit(solution)/shard_map/ppermute | solution.py:10
  126.3 113.5 %copy-start.6 = (bf16[4096,8]{0,1:T(8,128)(2,1)S(1)}, bf16[4096,8]{0,1:T(8,128)(2,1)}, u32[]{:S(2)}) copy-start(bf16[4096,8]{0,1:T(8,128)(2,1)} %param.7) | copy-start | bytes 196612
  126.4 77.4 %collective-permute-start.3 = (f32[768,128]{1,0:T(8,128)S(1)}, f32[768,128]{1,0:T(8,128)S(1)}, u32[]{:S(2)}, u32[]{:S(2)}) collective-permute-start(f32[768,128]{1,0:T(8,128)S(1)} %pad_maximum_fusion.5), channel_id=1, source_target_pairs={{0,32},{4,36},{8,40},{12,44},{16,48},{20,52},{24,56},{28,60},{32,0... | collective-permute-start | bytes 1179656 | tf_op jit(solution)/shard_map/ppermute | solution.py:10
  203.9 11.6 collective-permute-start.4
  215.6 5.8 collective-permute-start.5
  221.5 5.2 collective-permute-start.6
  242.2 680.6 %copy-start.7 = (bf16[16,4096]{1,0:T(8,128)(2,1)S(1)}, bf16[16,4096]{1,0:T(8,128)(2,1)}, u32[]{:S(2)}) copy-start(bf16[16,4096]{1,0:T(8,128)(2,1)} %param.9) | copy-start | bytes 393220
  242.2 683.0 %copy-start.5 = (bf16[4096,16]{0,1:T(8,128)(2,1)S(1)}, bf16[4096,16]{0,1:T(8,128)(2,1)}, u32[]{:S(2)}) copy-start(bf16[4096,16]{0,1:T(8,128)(2,1)} %param.8) | copy-start | bytes 393220
  242.2 680.6 %all-gather.2.cloned.1.call-start = ((), (), s32[]{:S(2)}) async-start(), calls=%async_computation.3 | async-start | bytes 2101248 | tf_op jit(solution)/shard_map/all_gather | solution.py:67
  727.2 198.0 %reduce-scatter.2.cloned.1.call-start = ((), (), s32[]{:S(2)}) async-start(), calls=%async_computation.2 | async-start | bytes 40960 | tf_op jit(solution)/shard_map/reduce_scatter | solution.py:60
  932.8 26.5 %collective-permute-start.7 = (f32[2048,128]{1,0:T(8,128)}, f32[2048,128]{1,0:T(8,128)S(1)}, u32[]{:S(2)}, u32[]{:S(2)}) collective-permute-start(f32[2048,128]{1,0:T(8,128)} %bitcast.8), channel_id=1, source_target_pairs={{0,128},{4,132},{8,136},{12,140},{16,144},{20,148},{24,152},{28,15... | collective-permute-start | bytes 3145736 | tf_op jit(solution)/shard_map/ppermute | solution.py:10
  961.4 46.4 %collective-permute-start.8 = (f32[1024,128]{1,0:T(8,128)S(1)}, f32[1024,128]{1,0:T(8,128)S(1)}, u32[]{:S(2)}, u32[]{:S(2)}) collective-permute-start(f32[1024,128]{1,0:T(8,128)S(1)} %bitcast.87), channel_id=1, source_target_pairs={{0,64},{4,68},{8,72},{12,76},{16,80},{20,84},{24,88},{28,92},{32,9... | collective-permute-start | bytes 1572872 | tf_op jit(solution)/shard_map/ppermute | solution.py:10
  1008.3 18.3 %collective-permute-start.9 = (f32[512,128]{1,0:T(8,128)S(1)}, f32[512,128]{1,0:T(8,128)S(1)}, u32[]{:S(2)}, u32[]{:S(2)}) collective-permute-start(f32[512,128]{1,0:T(8,128)S(1)} %bitcast.96), channel_id=1, source_target_pairs={{0,32},{4,36},{8,40},{12,44},{16,48},{20,52},{24,56},{28,60},{32,0... | collective-permute-start | bytes 786440 | tf_op jit(solution)/shard_map/ppermute | solution.py:10
  1026.8 20.5 %collective-permute-start.10 = (f32[256,128]{1,0:T(8,128)S(1)}, f32[256,128]{1,0:T(8,128)S(1)}, u32[]{:S(2)}, u32[]{:S(2)}) collective-permute-start(f32[256,128]{1,0:T(8,128)S(1)} %bitcast.97), channel_id=1, source_target_pairs={{0,16},{4,20},{8,24},{12,28},{16,0},{20,4},{24,8},{28,12},{32,48},... | collective-permute-start | bytes 393224 | tf_op jit(solution)/shard_map/ppermute | solution.py:10
  1047.4 5.0 collective-permute-start.11
  1052.5 10.4 collective-permute-start.12
  1074.4 6.9 collective-permute-start.13
  1081.4 5.0 collective-permute-start.14
  1086.5 10.5 collective-permute-start.15
  1097.3 28.5 %collective-permute-start.16 = (f32[512,128]{1,0:T(8,128)S(1)}, f32[512,128]{1,0:T(8,128)S(1)}, u32[]{:S(2)}, u32[]{:S(2)}) collective-permute-start(f32[512,128]{1,0:T(8,128)S(1)} %bitcast.85), channel_id=1, source_target_pairs={{0,32},{4,36},{8,40},{12,44},{16,48},{20,52},{24,56},{28,60},{32,0... | collective-permute-start | bytes 786440 | tf_op jit(solution)/shard_map/ppermute | solution.py:10
  1126.3 52.6 %collective-permute-start.17 = (f32[1024,128]{1,0:T(8,128)S(1)}, f32[1024,128]{1,0:T(8,128)S(1)}, u32[]{:S(2)}, u32[]{:S(2)}) collective-permute-start(f32[1024,128]{1,0:T(8,128)S(1)} %bitcast.80), channel_id=1, source_target_pairs={{0,64},{4,68},{8,72},{12,76},{16,80},{20,84},{24,88},{28,92},{32,9... | collective-permute-start | bytes 1572872 | tf_op jit(solution)/shard_map/ppermute | solution.py:10
  1179.8 26.1 %collective-permute-start.18 = (f32[2048,128]{1,0:T(8,128)S(1)}, f32[2048,128]{1,0:T(8,128)S(1)}, u32[]{:S(2)}, u32[]{:S(2)}) collective-permute-start(f32[2048,128]{1,0:T(8,128)S(1)} %bitcast.77), channel_id=1, source_target_pairs={{0,128},{4,132},{8,136},{12,140},{16,144},{20,148},{24,152},{28,15... | collective-permute-start | bytes 3145736 | tf_op jit(solution)/shard_map/ppermute | solution.py:10
Sparse Core Ops, SparseCore 0:
  242.3 481.5 all-reduce.2
  729.1 193.6 all-gather.1
Sparse Core Ops, SparseCore 1:
  730.5 23.3 reduce-scatter.1
where the time goes:
time: 1220 us
  waiting for transfers between devices  999 us (82%)
  starting transfers between devices  137 us (11%)
  blocking collectives  24.7 us (2%)
  local copies, waits for them, and re-layouts  17.6 us (1%)
  between operations  16.9 us (1%)
  matrix products  13.9 us (1%)
  other arithmetic  13.5 us (1%)
    psum x1, waiting for transfers between devices, body(): lax.psum(jnp.dot(top_factor, top_block, precision=lax.Precision.HIGHEST),...  482 us
    ppermute x19, waiting for transfers between devices, from_partner(): return lax.ppermute(value, axis, pairs)  323 us
    all_gather x1, waiting for transfers between devices, body(): lax.all_gather(top_adjoint, ('leaf', 'panel'), axis=0, tiled=True)  195 us
    ppermute x19, starting transfers between devices, from_partner(): return lax.ppermute(value, axis, pairs)  136 us
  transfers between devices with their start and end apart: 22, of which 20 were waited for; matrix products, arithmetic and copies ran while one was open for 0% of the time, Pallas kernels for 0%

commit v1 on v0

v1 whole, which is shorter than its diff:
```python
import functools

import jax
import jax.numpy as jnp
from jax import lax
from jax.experimental import pallas as pl
from jax.experimental.pallas import tpu as pltpu
from jax.sharding import PartitionSpec as P

CHIPS_Y = 4
CORES = 2
F32 = jnp.float32
BF16 = jnp.bfloat16


def dot_split(factor, value):
    high = value.astype(BF16)
    low = (value - high.astype(F32)).astype(BF16)
    return jnp.dot(factor, low, preferred_element_type=F32) + jnp.dot(
        factor, high, preferred_element_type=F32
    )


def kernel(
    dims,
    border, solution, top_factor, mid_factor, coupling,
    top_out, mid_out,
    border_send, border_land, sol_land,
    top_land, mid_land, couple_send, couple_land,
    top_y_send, top_y_land, mid_y_send, mid_y_land,
    load_send, load_land, load_own, load_all,
    inner_send, inner_land, inner_own, inner_all,
    adj_send, adj_land, adj_own, adj_all,
    rhs_send, rhs_land, rhs_own, rhs_all,
    minner_send, minner_land, minner_own, minner_all,
    madj_send, madj_land,
    send_sem, recv_sem,
):
    ny, nz, nx = dims
    nq = CORES * nx
    half = ny // 2
    leaf = lax.axis_index("leaf")
    x = lax.axis_index("panel")
    c = lax.rem(leaf, CORES)
    z = lax.rem(lax.div(leaf, CORES), nz)
    y = lax.div(leaf, CORES * nz)
    q = c * nx + x
    y_low = lax.rem(y, half)
    y_base = y - y_low

    def device(y_at, z_at, q_at):
        return ((y_at * nz + z_at) * CORES + lax.div(q_at, nx), lax.rem(q_at, nx))

    groups = {
        "q": (nq, q, lambda i: device(y, z, i)),
        "y": (ny, y, lambda i: device(i, z, q)),
        "pair": (half, y_low, lambda i: device(y_base + i, z, q)),
        "z": (nz, z, lambda i: device(y, i, q)),
        "plane": (ny * nq, y * nq + q, lambda i: device(lax.div(i, nq), z, lax.rem(i, nq))),
        "half": (
            half * nq,
            y_low * nq + q,
            lambda i: device(y_base + lax.div(i, nq), z, lax.rem(i, nq)),
        ),
    }
    pending = []

    def send(slot, group, source, landing):
        count, me, target = groups[group]

        def one(step, carry):
            peer = lax.rem(me + step, count)
            pltpu.make_async_remote_copy(
                src_ref=source(peer),
                dst_ref=landing.at[me],
                send_sem=send_sem.at[slot],
                recv_sem=recv_sem.at[slot],
                device_id=target(peer),
                device_id_type=pl.DeviceIdType.MESH,
            ).start()
            return carry

        lax.fori_loop(1, count, one, 0)
        others = landing.at[pl.ds(0, count - 1)]
        whole = pltpu.make_async_remote_copy(
            src_ref=others,
            dst_ref=others,
            send_sem=send_sem.at[slot],
            recv_sem=recv_sem.at[slot],
            device_id=target(lax.rem(me + 1, count)),
            device_id_type=pl.DeviceIdType.MESH,
        )
        pending.append(whole)
        return whole

    def scatter_sum(slot, group, buffer, landing):
        me = groups[group][1]
        whole = send(slot, group, lambda peer: buffer.at[peer], landing)
        landing[me] = buffer[me]
        whole.wait_recv()
        return jnp.sum(landing[...], axis=0)

    def gather(slot, group, own, landing):
        me = groups[group][1]
        whole = send(slot, group, lambda peer: own, landing)
        landing[me] = own[...]
        whole.wait_recv()
        value = landing[...]
        return value.reshape(-1, value.shape[-1])

    barrier = pltpu.get_barrier_semaphore()
    for name in ("plane", "z"):
        count, me, target = groups[name]

        def greet(step, carry, count=count, me=me, target=target):
            pl.semaphore_signal(
                barrier,
                inc=1,
                device_id=target(lax.rem(me + step, count)),
                device_id_type=pl.DeviceIdType.MESH,
            )
            return carry

        lax.fori_loop(1, count, greet, 0)

    rows = border.shape[0]
    top_rows = top_out.shape[0]
    mid_rows = mid_out.shape[0]
    block = nz * nq * top_rows
    lanes = nz * top_rows
    source_id = lax.broadcasted_iota(jnp.int32, (block, lanes), 0)
    lane_id = lax.broadcasted_iota(jnp.int32, (block, lanes), 1)
    for part, owned in ((0, top_rows), (1, mid_rows)):
        first = part * ny
        stacked = jnp.concatenate(
            [border[:, (first + b) * block : (first + b + 1) * block] for b in range(ny)], 0
        )
        offset = source_id - (
            lax.div(lane_id, owned) * (nq * owned) + lax.rem(lane_id, owned)
        )

        def pick(at, carry, stacked=stacked, offset=offset, owned=owned, first=first):
            chosen = jnp.where(offset == at * owned, 1.0, 0.0).astype(BF16)
            moved = jnp.dot(stacked, chosen, preferred_element_type=F32)
            border_send[at, pl.ds(first, ny)] = moved.reshape(ny, rows, lanes)
            return carry

        lax.fori_loop(0, nq, pick, 0)

    seg = nq * top_rows
    low_half = lax.broadcasted_iota(jnp.int32, (mid_rows, 2 * seg), 1) < seg
    for z_at in range(nz):
        for pair in range(ny // 2):
            tiles = []
            for y_at in (2 * pair, 2 * pair + 1):
                start = (y_at * nz + z_at - z_at % 2) * seg
                tiles.append(coupling[:, start : start + 2 * seg].astype(F32))
            if z_at % 2 == 0:
                tiles[1] = pltpu.roll(tiles[1], seg, 1)
            else:
                tiles[0] = pltpu.roll(tiles[0], seg, 1)
            couple_send[z_at, :, pair * 2 * seg : (pair + 1) * 2 * seg] = jnp.where(
                low_half, tiles[0], tiles[1]
            )

    pl.semaphore_wait(barrier, ny * nq + nz - 2)

    sol_wait = send(0, "q", lambda peer: solution, sol_land)
    border_wait = send(1, "q", lambda peer: border_send.at[peer], border_land)
    width = top_factor.shape[1] // nz

    def columns(ref):
        return lambda peer: ref.at[:, pl.ds(pl.multiple_of(peer * width, width), width)]

    top_wait = send(2, "z", columns(top_factor), top_land)
    couple_wait = send(3, "z", lambda peer: couple_send.at[peer], couple_land)
    mid_wait = send(4, "z", columns(mid_factor), mid_land)
    sol_land[q] = solution[...]
    border_land[q] = border_send[q]
    own_columns = pl.ds(pl.multiple_of(z * width, width), width)
    top_land[z] = top_factor[:, own_columns]
    mid_land[z] = mid_factor[:, own_columns]
    couple_land[z] = couple_send[z]

    sol_wait.wait_recv()
    border_wait.wait_recv()
    loads = sol_land[...].reshape(nq * rows, -1).astype(BF16)

    def load_block(b):
        part = border_land[:, b].reshape(nq * rows, lanes)
        return jnp.dot(part.T.astype(BF16), loads, preferred_element_type=F32)

    for b in range(ny):
        top_y_send[b] = load_block(b)
    per_half = ny // half
    top_y_wait = send(5, "y", lambda peer: top_y_send.at[peer], top_y_land)
    for b in range(ny):
        mid_y_send[b // per_half, (b % per_half) * lanes : (b % per_half + 1) * lanes] = load_block(
            ny + b
        )
    mid_y_wait = send(6, "pair", lambda peer: mid_y_send.at[peer], mid_y_land)
    top_y_land[y] = top_y_send[y]
    mid_y_land[y_low] = mid_y_send[y_low]

    top_wait.wait_recv()
    top_t = top_land[...].reshape(nz * top_rows, width)
    top_w = top_t.T.astype(BF16)
    top_t = top_t.astype(BF16)

    top_y_wait.wait_recv()
    load_send[...] = jnp.sum(top_y_land[...], axis=0).reshape(load_send.shape)
    load_own[...] = scatter_sum(7, "z", load_send, load_land)
    top_load = gather(8, "z", load_own, load_all)

    inner_send[...] = dot_split(top_w, top_load).reshape(inner_send.shape)
    inner_own[...] = scatter_sum(9, "plane", inner_send, inner_land)
    top_inner = gather(10, "plane", inner_own, inner_all)

    adj_send[...] = dot_split(top_t, top_inner).reshape(adj_send.shape)
    adjoint = scatter_sum(11, "z", adj_send, adj_land)
    adj_own[...] = adjoint
    top_out[...] = adjoint
    top_block = gather(12, "plane", adj_own, adj_all)

    couple_wait.wait_recv()
    couple = couple_land[...].reshape(nz * mid_rows, width).astype(BF16)
    mid_y_wait.wait_recv()
    mid_load = jnp.sum(mid_y_land[...], axis=0)
    rhs_send[...] = (mid_load - dot_split(couple, top_block)).reshape(rhs_send.shape)
    rhs_own[...] = scatter_sum(13, "z", rhs_send, rhs_land)
    mid_wait.wait_recv()
    mid_t = mid_land[...].reshape(nz * mid_rows, width)
    mid_w = mid_t.T.astype(BF16)
    mid_t = mid_t.astype(BF16)
    mid_rhs = gather(14, "z", rhs_own, rhs_all)

    minner_send[...] = dot_split(mid_w, mid_rhs).reshape(minner_send.shape)
    minner_own[...] = scatter_sum(15, "half", minner_send, minner_land)
    mid_inner = gather(16, "half", minner_own, minner_all)

    madj_send[...] = dot_split(mid_t, mid_inner).reshape(madj_send.shape)
    mid_out[...] = scatter_sum(17, "z", madj_send, madj_land)

    for whole in pending:
        whole.wait_send()


def body(dims, border, solution, winv_top, winv_mid, coupling):
    ny, nz, nx = dims
    nq = CORES * nx
    half = ny // 2
    rows, width = border.shape[1:]
    loads = solution.shape[2]
    top_rows = winv_top.shape[1]
    mid_rows = winv_mid.shape[1]
    front = winv_top.shape[0]
    z_width = front // nz

    def buf(*shape):
        return pltpu.VMEM(shape, F32)

    def exchange(count, height):
        return [buf(count, height, loads), buf(count, height, loads)]

    def reduce_gather(count, height):
        return exchange(count, height) + [buf(height, loads), buf(count, height, loads)]

    plane = ny * nq
    scratch = (
        [buf(nq, 2 * ny, rows, nz * top_rows)] * 2
        + [buf(nq, rows, loads)]
        + [buf(nz, top_rows, z_width), buf(nz, mid_rows, z_width)]
        + [buf(nz, mid_rows, z_width)] * 2
        + exchange(ny, nz * top_rows)
        + exchange(half, nz * mid_rows)
        + reduce_gather(nz, top_rows)
        + reduce_gather(plane, z_width // plane)
        + [buf(nz, top_rows, loads)] * 2
        + [buf(top_rows, loads), buf(plane, top_rows, loads)]
        + reduce_gather(nz, mid_rows)
        + reduce_gather(half * nq, z_width // (half * nq))
        + exchange(nz, mid_rows)
        + [pltpu.SemaphoreType.DMA((18,)), pltpu.SemaphoreType.DMA((18,))]
    )
    vmem = pl.BlockSpec(memory_space=pltpu.VMEM)
    return pl.pallas_call(
        functools.partial(kernel, dims),
        out_shape=(
            jax.ShapeDtypeStruct((top_rows, loads), F32),
            jax.ShapeDtypeStruct((mid_rows, loads), F32),
        ),
        in_specs=[vmem] * 5,
        out_specs=(vmem, vmem),
        scratch_shapes=scratch,
        compiler_params=pltpu.CompilerParams(collective_id=0, has_side_effects=True),
        name="adjoint",
    )(
        border[0],
        solution[0].astype(F32),
        winv_top.T.astype(F32),
        winv_mid.T.astype(F32),
        coupling,
    )


def solution(mesh, chips_y=CHIPS_Y):
    placed = (
        P("leaf", "panel", None),
        P("leaf", "panel", None),
        P(None, ("leaf", "panel")),
        P(None, ("leaf", "panel")),
        P(("leaf", "panel"), None),
    )
    dims = (chips_y, mesh.shape["leaf"] // (CORES * chips_y), mesh.shape["panel"])
    return jax.shard_map(
        functools.partial(body, dims),
        mesh=mesh,
        in_specs=placed,
        out_specs=(P(("leaf", "panel"), None), P(("leaf", "panel"), None)),
        check_vma=False,
    )
```

time: 1220 us -> 138 us (0.11)
  waiting for transfers between devices: 999 us -> 0 us
  starting transfers between devices: 137 us -> 0 us
  Pallas kernels: 0 us -> 132 us
  blocking collectives: 24.7 us -> 0 us
  between operations: 16.9 us -> 0.66 us
  local copies, waits for them, and re-layouts: 17.6 us -> 1.89 us
  matrix products: 13.9 us -> 0 us
    psum x1 -> x0, waiting for transfers between devices: 482 us -> none  [body(): lax.psum(jnp.dot(top_factor, top_block, precision=lax.Precision.HIGHEST),...]
    ppermute x19 -> x0, waiting for transfers between devices: 323 us -> none  [from_partner(): return lax.ppermute(value, axis, pairs)]
    all_gather x1 -> x0, waiting for transfers between devices: 195 us -> none  [body(): lax.all_gather(top_adjoint, ('leaf', 'panel'), axis=0, tiled=True)]
    ppermute x19 -> x0, starting transfers between devices: 136 us -> none  [from_partner(): return lax.ppermute(value, axis, pairs)]
    pallas_call x0 -> x1, Pallas kernels: none -> 132 us  [body(): pl.pallas_call(functools.partial(kernel, dims), out_shape=(jax.ShapeDtype...]
    dot_general x6 -> x0, matrix products: 13.9 us -> none  [the longest x1 3.23 us: body(): jnp.dot(top_factor.T, top_inner, precision=lax.Precision.HIGHEST)]
    unnamed x1 -> x0, blocking collectives: 13.1 us -> none
  transfers between devices with their start and end apart: 22 -> 0, of which waited for: 20 -> 0; matrix products, arithmetic and copies ran while one was open for 0% -> 0% of each run, Pallas kernels for 0% -> 0%
where the time goes in v1:
time: 138 us
  Pallas kernels  132 us (96%)
  other arithmetic  3.55 us (3%)
  local copies, waits for them, and re-layouts  1.89 us (1%)
    pallas_call x1, Pallas kernels, body(): pl.pallas_call(functools.partial(kernel, dims), out_shape=(jax.ShapeDtype...  132 us

profile of v1, /device:TPU:1, one launch (start us, length us, event | category | flops | bytes accessed | tf_op | source)
XLA Modules:
  0.0 138.2 jit_solution(9880536722752359663)
XLA Ops:
  0.6 0.0 copy-start
  0.6 1.3 bitcast_convert_fusion.solution
  2.0 1.5 %convert_bitcast_fusion.1.top_factor = f32[8,4096]{1,0:T(8,128)} fusion(bf16[4096,8]{0,1:T(8,128)(2,1)} %param.7), kind=kLoop, calls=%fused_computation.1 | loop fusion | flops 32768 | bytes 196608 | tf_op jit(solution)/shard_map/convert_element_type | solution.py:300
  3.5 0.0 copy-done
  3.5 0.7 convert_bitcast_fusion.mid_factor
  4.2 132.1 %adjoint.1 = (f32[8,128]{1,0:T(8,128)}, f32[16,128]{1,0:T(8,128)}) custom-call(bf16[32,8192]{1,0:T(8,128)(2,1)} %bitcast.8, f32[32,128]{1,0:T(8,128)} %bitcast_convert_fusion.solution, f32[8,4096]{1,0:T(8,128)} %convert_bitcast_fusion.1.top_factor, f32[16,4096]{1,0:T(8,128)} %convert_bitcast_fusion.mid_factor, bf16[16,4096]{1,0:T(8,128)(2,1)} %coupling.1), custom_call_target="tpu_custom_call" | custom-call | tf_op jit(solution)/shard_map/adjoint/pallas_call | solution.py:286
  136.3 0.0 copy-start.1
  136.3 1.3 copy.9
  137.6 0.0 copy-done.1
  137.6 0.6 copy.10
Async XLA Ops:
  0.6 2.9 %copy-start = (bf16[4096,16]{0,1:T(8,128)(2,1)S(1)}, bf16[4096,16]{0,1:T(8,128)(2,1)}, u32[]{:S(2)}) copy-start(bf16[4096,16]{0,1:T(8,128)(2,1)} %param.8) | copy-start | bytes 393220
  136.3 1.3 copy-start.1

commit v2 on v1

--- a/solution.py
+++ b/solution.py
@@ -25,8 +25,8 @@
     dims,
     border, solution, top_factor, mid_factor, coupling,
     top_out, mid_out,
-    border_send, border_land, sol_land,
-    top_land, mid_land, couple_send, couple_land,
+    border_send, border_land, sol_send, sol_land, sol_blocks,
+    top_send, top_land, mid_send, mid_land, couple_send, couple_land,
     top_y_send, top_y_land, mid_y_send, mid_y_land,
     load_send, load_land, load_own, load_all,
     inner_send, inner_land, inner_own, inner_all,
@@ -128,24 +128,31 @@
     mid_rows = mid_out.shape[0]
     block = nz * nq * top_rows
     lanes = nz * top_rows
-    source_id = lax.broadcasted_iota(jnp.int32, (block, lanes), 0)
-    lane_id = lax.broadcasted_iota(jnp.int32, (block, lanes), 1)
+    width = top_factor.shape[1] // nz
+    sol_send[...] = solution[...].astype(F32)
+    top_send[...] = top_factor[...].astype(F32)
     for part, owned in ((0, top_rows), (1, mid_rows)):
         first = part * ny
         stacked = jnp.concatenate(
             [border[:, (first + b) * block : (first + b + 1) * block] for b in range(ny)], 0
         )
-        offset = source_id - (
-            lax.div(lane_id, owned) * (nq * owned) + lax.rem(lane_id, owned)
-        )
-
-        def pick(at, carry, stacked=stacked, offset=offset, owned=owned, first=first):
-            chosen = jnp.where(offset == at * owned, 1.0, 0.0).astype(BF16)
-            moved = jnp.dot(stacked, chosen, preferred_element_type=F32)
-            border_send[at, pl.ds(first, ny)] = moved.reshape(ny, rows, lanes)
-            return carry
-
-        lax.fori_loop(0, nq, pick, 0)
+        turned = stacked.astype(F32).T.reshape(block // (nq * owned), nq, owned, ny * rows)
+        for q_at in range(nq):
+            border_send[q_at, part] = turned[:, q_at].reshape(lanes, ny * rows)
+    sol_blocks[...] = jnp.zeros_like(sol_blocks)
+
+    pl.semaphore_wait(barrier, ny * nq + nz - 2)
+
+    def columns(ref):
+        return lambda peer: ref.at[:, pl.ds(pl.multiple_of(peer * width, width), width)]
+
+    own_columns = pl.ds(pl.multiple_of(z * width, width), width)
+    sol_wait = send(0, "q", lambda peer: sol_send, sol_land)
+    border_wait = send(1, "q", lambda peer: border_send.at[peer], border_land)
+    top_wait = send(2, "z", columns(top_send), top_land)
+    sol_land[q] = sol_send[...]
+    border_land[q] = border_send[q]
+    top_land[z] = top_send[:, own_columns]
 
     seg = nq * top_rows
     low_half = lax.broadcasted_iota(jnp.int32, (mid_rows, 2 * seg), 1) < seg
@@ -163,41 +170,40 @@
                 low_half, tiles[0], tiles[1]
             )
 
-    pl.semaphore_wait(barrier, ny * nq + nz - 2)
-
-    sol_wait = send(0, "q", lambda peer: solution, sol_land)
-    border_wait = send(1, "q", lambda peer: border_send.at[peer], border_land)
-    width = top_factor.shape[1] // nz
-
-    def columns(ref):
-        return lambda peer: ref.at[:, pl.ds(pl.multiple_of(peer * width, width), width)]
-
-    top_wait = send(2, "z", columns(top_factor), top_land)
     couple_wait = send(3, "z", lambda peer: couple_send.at[peer], couple_land)
-    mid_wait = send(4, "z", columns(mid_factor), mid_land)
-    sol_land[q] = solution[...]
-    border_land[q] = border_send[q]
-    own_columns = pl.ds(pl.multiple_of(z * width, width), width)
-    top_land[z] = top_factor[:, own_columns]
-    mid_land[z] = mid_factor[:, own_columns]
     couple_land[z] = couple_send[z]
+    mid_send[...] = mid_factor[...].astype(F32)
+    mid_land[z] = mid_send[:, own_columns]
 
     sol_wait.wait_recv()
+    columns_out = sol_send.shape[1]
+    for source in range(nq):
+        part = sol_land[source].astype(BF16)
+        for b in range(ny):
+            sol_blocks[
+                source,
+                b * rows : (b + 1) * rows,
+                b * columns_out : (b + 1) * columns_out,
+            ] = part
     border_wait.wait_recv()
-    loads = sol_land[...].reshape(nq * rows, -1).astype(BF16)
-
-    def load_block(b):
-        part = border_land[:, b].reshape(nq * rows, lanes)
-        return jnp.dot(part.T.astype(BF16), loads, preferred_element_type=F32)
-
-    for b in range(ny):
-        top_y_send[b] = load_block(b)
+
+    def loads(part):
+        total = None
+        for source in range(0, nq, 2):
+            left = jnp.concatenate(
+                [border_land[source, part], border_land[source + 1, part]], 1
+            ).astype(BF16)
+            right = sol_blocks[source : source + 2].reshape(2 * ny * rows, -1)
+            term = jnp.dot(left, right, preferred_element_type=F32)
+            total = term if total is None else total + term
+        return [total[:, b * columns_out : (b + 1) * columns_out] for b in range(ny)]
+
+    for b, value in enumerate(loads(0)):
+        top_y_send[b] = value
     per_half = ny // half
     top_y_wait = send(5, "y", lambda peer: top_y_send.at[peer], top_y_land)
-    for b in range(ny):
-        mid_y_send[b // per_half, (b % per_half) * lanes : (b % per_half + 1) * lanes] = load_block(
-            ny + b
-        )
+    for b, value in enumerate(loads(1)):
+        mid_y_send[b // per_half, (b % per_half) * lanes : (b % per_half + 1) * lanes] = value
     mid_y_wait = send(6, "pair", lambda peer: mid_y_send.at[peer], mid_y_land)
     top_y_land[y] = top_y_send[y]
     mid_y_land[y_low] = mid_y_send[y_low]
@@ -211,6 +217,7 @@
     load_send[...] = jnp.sum(top_y_land[...], axis=0).reshape(load_send.shape)
     load_own[...] = scatter_sum(7, "z", load_send, load_land)
     top_load = gather(8, "z", load_own, load_all)
+    mid_wait = send(4, "z", columns(mid_send), mid_land)
 
     inner_send[...] = dot_split(top_w, top_load).reshape(inner_send.shape)
     inner_own[...] = scatter_sum(9, "plane", inner_send, inner_land)
@@ -267,9 +274,11 @@
 
     plane = ny * nq
     scratch = (
-        [buf(nq, 2 * ny, rows, nz * top_rows)] * 2
-        + [buf(nq, rows, loads)]
-        + [buf(nz, top_rows, z_width), buf(nz, mid_rows, z_width)]
+        [buf(nq, 2, nz * top_rows, ny * rows)] * 2
+        + [buf(rows, loads), buf(nq, rows, loads)]
+        + [pltpu.VMEM((nq, ny * rows, ny * loads), BF16)]
+        + [buf(top_rows, front), buf(nz, top_rows, z_width)]
+        + [buf(mid_rows, front), buf(nz, mid_rows, z_width)]
         + [buf(nz, mid_rows, z_width)] * 2
         + exchange(ny, nz * top_rows)
         + exchange(half, nz * mid_rows)
@@ -296,9 +305,9 @@
         name="adjoint",
     )(
         border[0],
-        solution[0].astype(F32),
-        winv_top.T.astype(F32),
-        winv_mid.T.astype(F32),
+        solution[0],
+        winv_top.T,
+        winv_mid.T,
         coupling,
     )
 

time: 138 us -> 125 us (0.906)
  Pallas kernels: 132 us -> 122 us
  other arithmetic: 3.55 us -> 0 us
    pallas_call x1, Pallas kernels: 132 us -> 122 us  [body(): pl.pallas_call(functools.partial(kernel, dims), out_shape=(jax.ShapeDtype...]
    convert_element_type x3 -> x0, other arithmetic: 3.55 us -> none  [the longest x1 1.52 us: body(): winv_top.T.astype(F32)]
where the time goes in v2:
time: 125 us
  Pallas kernels  122 us (98%)
  local copies, waits for them, and re-layouts  1.88 us (2%)
    pallas_call x1, Pallas kernels, body(): pl.pallas_call(functools.partial(kernel, dims), out_shape=(jax.ShapeDtype...  122 us

profile of v2, /device:TPU:1, one launch (start us, length us, event | category | flops | bytes accessed | tf_op | source)
XLA Modules:
  0.0 124.6 jit_solution(5966310197623011818)
XLA Ops:
  0.6 122.0 %adjoint.1 = (f32[8,128]{1,0:T(8,128)}, f32[16,128]{1,0:T(8,128)}) custom-call(bf16[32,8192]{1,0:T(8,128)(2,1)} %bitcast.4, bf16[32,128]{1,0:T(8,128)(2,1)} %bitcast.7, bf16[8,4096]{1,0:T(8,128)(2,1)} %bitcast.6, bf16[16,4096]{1,0:T(8,128)(2,1)} %bitcast.5, bf16[16,4096]{1,0:T(8,128)(2,1)} %coupling.1), custom_call_target="tpu_custom_call" | custom-call | tf_op jit(solution)/shard_map/adjoint/pallas_call | solution.py:295
  122.7 0.0 copy-start
  122.7 1.3 %copy.9 = f32[8,128]{1,0:T(8,128)} copy(f32[8,128]{1,0:T(8,128)} %get-tuple-element.4) | data formatting | bytes 8192
  124.0 0.0 copy-done
  124.0 0.6 copy.10
Async XLA Ops:
  122.7 1.3 %copy-start = (f32[16,128]{1,0:T(8,128)S(1)}, f32[16,128]{1,0:T(8,128)}, u32[]{:S(2)}) copy-start(f32[16,128]{1,0:T(8,128)} %get-tuple-element.5) | copy-start | bytes 24580

commit v3 on v2

--- a/solution.py
+++ b/solution.py
@@ -48,80 +48,89 @@
     y_low = lax.rem(y, half)
     y_base = y - y_low
 
-    def device(y_at, z_at, q_at):
-        return ((y_at * nz + z_at) * CORES + lax.div(q_at, nx), lax.rem(q_at, nx))
+    def ring(me, count):
+        steps = sorted(range(1, count), key=lambda step: -min(step, count - step))
+        return [lax.rem(me + step, count) for step in steps]
+
+    def leaf_of(y_at, z_at, c_at):
+        return (y_at * nz + z_at) * CORES + c_at
+
+    xs, zs, ys, lows = ring(x, nx), ring(z, nz), ring(y, ny), ring(y_low, half)
+    flips = [1 - c]
+
+    def sheet(me, others, base):
+        return [
+            (y_at * nq + c_at * nx + x_at, (leaf_of(base + y_at, z, c_at), x_at))
+            for y_at in others + [me]
+            for x_at in xs + [x]
+            for c_at in flips + [c]
+        ][:-1]
 
     groups = {
-        "q": (nq, q, lambda i: device(y, z, i)),
-        "y": (ny, y, lambda i: device(i, z, q)),
-        "pair": (half, y_low, lambda i: device(y_base + i, z, q)),
-        "z": (nz, z, lambda i: device(y, i, q)),
-        "plane": (ny * nq, y * nq + q, lambda i: device(lax.div(i, nq), z, lax.rem(i, nq))),
-        "half": (
-            half * nq,
-            y_low * nq + q,
-            lambda i: device(y_base + lax.div(i, nq), z, lax.rem(i, nq)),
-        ),
+        "q": (nq, q, [(c_at * nx + x_at, (leaf_of(y, z, c_at), x_at)) for x_at in xs + [x] for c_at in flips + [c]][:-1]),
+        "y": (ny, y, [(y_at, (leaf_of(y_at, z, c), x)) for y_at in ys]),
+        "pair": (half, y_low, [(low, (leaf_of(y_base + low, z, c), x)) for low in lows]),
+        "z": (nz, z, [(z_at, (leaf_of(y, z_at, c), x)) for z_at in zs]),
+        "plane": (ny * nq, y * nq + q, sheet(y, ys, 0)),
+        "half": (half * nq, y_low * nq + q, sheet(y_low, lows, y_base)),
     }
     pending = []
 
-    def send(slot, group, source, landing):
-        count, me, target = groups[group]
-
-        def one(step, carry):
-            peer = lax.rem(me + step, count)
+    def push(slot, group, source, landing, peers):
+        me = groups[group][1]
+        for peer, target in peers:
             pltpu.make_async_remote_copy(
                 src_ref=source(peer),
                 dst_ref=landing.at[me],
                 send_sem=send_sem.at[slot],
                 recv_sem=recv_sem.at[slot],
-                device_id=target(peer),
+                device_id=target,
                 device_id_type=pl.DeviceIdType.MESH,
             ).start()
-            return carry
-
-        lax.fori_loop(1, count, one, 0)
+
+    def waiter(slot, group, landing):
+        count, me, peers = groups[group]
         others = landing.at[pl.ds(0, count - 1)]
         whole = pltpu.make_async_remote_copy(
             src_ref=others,
             dst_ref=others,
             send_sem=send_sem.at[slot],
             recv_sem=recv_sem.at[slot],
-            device_id=target(lax.rem(me + 1, count)),
+            device_id=peers[0][1],
             device_id_type=pl.DeviceIdType.MESH,
         )
         pending.append(whole)
         return whole
 
-    def scatter_sum(slot, group, buffer, landing):
+    def send(slot, group, source, landing):
+        push(slot, group, source, landing, groups[group][2])
+        return waiter(slot, group, landing)
+
+    def scatter_sum(slot, group, buffer, landing, between=None):
         me = groups[group][1]
         whole = send(slot, group, lambda peer: buffer.at[peer], landing)
         landing[me] = buffer[me]
+        if between is not None:
+            between()
         whole.wait_recv()
         return jnp.sum(landing[...], axis=0)
 
-    def gather(slot, group, own, landing):
+    def gather(slot, group, own, landing, between=None):
         me = groups[group][1]
         whole = send(slot, group, lambda peer: own, landing)
         landing[me] = own[...]
+        if between is not None:
+            between()
         whole.wait_recv()
         value = landing[...]
         return value.reshape(-1, value.shape[-1])
 
     barrier = pltpu.get_barrier_semaphore()
-    for name in ("plane", "z"):
-        count, me, target = groups[name]
-
-        def greet(step, carry, count=count, me=me, target=target):
+    for name in ("z", "plane"):
+        for peer, target in groups[name][2]:
             pl.semaphore_signal(
-                barrier,
-                inc=1,
-                device_id=target(lax.rem(me + step, count)),
-                device_id_type=pl.DeviceIdType.MESH,
+                barrier, inc=1, device_id=target, device_id_type=pl.DeviceIdType.MESH
             )
-            return carry
-
-        lax.fori_loop(1, count, greet, 0)
 
     rows = border.shape[0]
     top_rows = top_out.shape[0]
@@ -131,16 +140,17 @@
     width = top_factor.shape[1] // nz
     sol_send[...] = solution[...].astype(F32)
     top_send[...] = top_factor[...].astype(F32)
-    for part, owned in ((0, top_rows), (1, mid_rows)):
+
+    def regroup(part, owned):
         first = part * ny
         stacked = jnp.concatenate(
             [border[:, (first + b) * block : (first + b + 1) * block] for b in range(ny)], 0
         )
         turned = stacked.astype(F32).T.reshape(block // (nq * owned), nq, owned, ny * rows)
         for q_at in range(nq):
-            border_send[q_at, part] = turned[:, q_at].reshape(lanes, ny * rows)
-    sol_blocks[...] = jnp.zeros_like(sol_blocks)
-
+            border_send[part, q_at] = turned[:, q_at].reshape(lanes, ny * rows)
+
+    regroup(0, top_rows)
     pl.semaphore_wait(barrier, ny * nq + nz - 2)
 
     def columns(ref):
@@ -148,10 +158,17 @@
 
     own_columns = pl.ds(pl.multiple_of(z * width, width), width)
     sol_wait = send(0, "q", lambda peer: sol_send, sol_land)
-    border_wait = send(1, "q", lambda peer: border_send.at[peer], border_land)
-    top_wait = send(2, "z", columns(top_send), top_land)
+    border_wait = send(1, "q", lambda peer: border_send.at[0, peer], border_land.at[0])
+    near = groups["z"][2][::-1]
+    early, late = near[: 2 * len(near) // 3], near[2 * len(near) // 3 :]
+    push(2, "z", columns(top_send), top_land, near)
+    top_wait = waiter(2, "z", top_land)
+    regroup(1, mid_rows)
+    border_mid_wait = send(18, "q", lambda peer: border_send.at[1, peer], border_land.at[1])
     sol_land[q] = sol_send[...]
-    border_land[q] = border_send[q]
+    border_land[0, q] = border_send[0, q]
+    border_land[1, q] = border_send[1, q]
+    sol_blocks[...] = jnp.zeros_like(sol_blocks)
     top_land[z] = top_send[:, own_columns]
 
     seg = nq * top_rows
@@ -170,7 +187,9 @@
                 low_half, tiles[0], tiles[1]
             )
 
-    couple_wait = send(3, "z", lambda peer: couple_send.at[peer], couple_land)
+    couple_rows = lambda peer: couple_send.at[peer]
+    push(3, "z", couple_rows, couple_land, early)
+    couple_wait = waiter(3, "z", couple_land)
     couple_land[z] = couple_send[z]
     mid_send[...] = mid_factor[...].astype(F32)
     mid_land[z] = mid_send[:, own_columns]
@@ -191,7 +210,7 @@
         total = None
         for source in range(0, nq, 2):
             left = jnp.concatenate(
-                [border_land[source, part], border_land[source + 1, part]], 1
+                [border_land[part, source], border_land[part, source + 1]], 1
             ).astype(BF16)
             right = sol_blocks[source : source + 2].reshape(2 * ny * rows, -1)
             term = jnp.dot(left, right, preferred_element_type=F32)
@@ -202,11 +221,27 @@
         top_y_send[b] = value
     per_half = ny // half
     top_y_wait = send(5, "y", lambda peer: top_y_send.at[peer], top_y_land)
-    for b, value in enumerate(loads(1)):
-        mid_y_send[b // per_half, (b % per_half) * lanes : (b % per_half + 1) * lanes] = value
-    mid_y_wait = send(6, "pair", lambda peer: mid_y_send.at[peer], mid_y_land)
     top_y_land[y] = top_y_send[y]
-    mid_y_land[y_low] = mid_y_send[y_low]
+
+    def mid_loads():
+        border_mid_wait.wait_recv()
+        for b, value in enumerate(loads(1)):
+            mid_y_send[
+                b // per_half, (b % per_half) * lanes : (b % per_half + 1) * lanes
+            ] = value
+        push(6, "pair", lambda peer: mid_y_send.at[peer], mid_y_land, groups["pair"][2])
+        mid_y_land[y_low] = mid_y_send[y_low]
+
+    mid_y_wait = waiter(6, "pair", mid_y_land)
+
+    def factors_early():
+        push(3, "z", couple_rows, couple_land, late)
+        push(4, "z", columns(mid_send), mid_land, early)
+
+    def factors_late():
+        push(4, "z", columns(mid_send), mid_land, late)
+
+    mid_wait = waiter(4, "z", mid_land)
 
     top_wait.wait_recv()
     top_t = top_land[...].reshape(nz * top_rows, width)
@@ -216,18 +251,17 @@
     top_y_wait.wait_recv()
     load_send[...] = jnp.sum(top_y_land[...], axis=0).reshape(load_send.shape)
     load_own[...] = scatter_sum(7, "z", load_send, load_land)
-    top_load = gather(8, "z", load_own, load_all)
-    mid_wait = send(4, "z", columns(mid_send), mid_land)
+    top_load = gather(8, "z", load_own, load_all, mid_loads)
 
     inner_send[...] = dot_split(top_w, top_load).reshape(inner_send.shape)
-    inner_own[...] = scatter_sum(9, "plane", inner_send, inner_land)
+    inner_own[...] = scatter_sum(9, "plane", inner_send, inner_land, factors_early)
     top_inner = gather(10, "plane", inner_own, inner_all)
 
     adj_send[...] = dot_split(top_t, top_inner).reshape(adj_send.shape)
     adjoint = scatter_sum(11, "z", adj_send, adj_land)
     adj_own[...] = adjoint
     top_out[...] = adjoint
-    top_block = gather(12, "plane", adj_own, adj_all)
+    top_block = gather(12, "plane", adj_own, adj_all, factors_late)
 
     couple_wait.wait_recv()
     couple = couple_land[...].reshape(nz * mid_rows, width).astype(BF16)
@@ -274,7 +308,7 @@
 
     plane = ny * nq
     scratch = (
-        [buf(nq, 2, nz * top_rows, ny * rows)] * 2
+        [buf(2, nq, nz * top_rows, ny * rows)] * 2
         + [buf(rows, loads), buf(nq, rows, loads)]
         + [pltpu.VMEM((nq, ny * rows, ny * loads), BF16)]
         + [buf(top_rows, front), buf(nz, top_rows, z_width)]
@@ -289,7 +323,7 @@
         + reduce_gather(nz, mid_rows)
         + reduce_gather(half * nq, z_width // (half * nq))
         + exchange(nz, mid_rows)
-        + [pltpu.SemaphoreType.DMA((18,)), pltpu.SemaphoreType.DMA((18,))]
+        + [pltpu.SemaphoreType.DMA((19,)), pltpu.SemaphoreType.DMA((19,))]
     )
     vmem = pl.BlockSpec(memory_space=pltpu.VMEM)
     return pl.pallas_call(

time: 125 us -> 110 us (0.88)
  Pallas kernels: 122 us -> 106 us
    pallas_call x1, Pallas kernels: 122 us -> 106 us  [body(): pl.pallas_call(functools.partial(kernel, dims), out_shape=(jax.ShapeDtype...]
where the time goes in v3:
time: 110 us; the launch traced here: 109 us
  Pallas kernels  106 us (96%)
  local copies, waits for them, and re-layouts  1.88 us (2%)
    pallas_call x1, Pallas kernels, body(): pl.pallas_call(functools.partial(kernel, dims), out_shape=(jax.ShapeDtype...  106 us

profile of v3, /device:TPU:1, one launch (start us, length us, event | category | flops | bytes accessed | tf_op | source)
XLA Modules:
  0.0 108.7 jit_solution(17462827607336952327)
XLA Ops:
  0.6 106.1 %adjoint.1 = (f32[8,128]{1,0:T(8,128)}, f32[16,128]{1,0:T(8,128)}) custom-call(bf16[32,8192]{1,0:T(8,128)(2,1)} %bitcast.4, bf16[32,128]{1,0:T(8,128)(2,1)} %bitcast.7, bf16[8,4096]{1,0:T(8,128)(2,1)} %bitcast.6, bf16[16,4096]{1,0:T(8,128)(2,1)} %bitcast.5, bf16[16,4096]{1,0:T(8,128)(2,1)} %coupling.1), custom_call_target="tpu_custom_call" | custom-call | tf_op jit(solution)/shard_map/adjoint/pallas_call | solution.py:329
  106.8 0.0 copy-start
  106.8 1.3 %copy.9 = f32[8,128]{1,0:T(8,128)} copy(f32[8,128]{1,0:T(8,128)} %get-tuple-element.4) | data formatting | bytes 8192
  108.1 0.0 copy-done
  108.1 0.6 copy.10
Async XLA Ops:
  106.8 1.3 %copy-start = (f32[16,128]{1,0:T(8,128)S(1)}, f32[16,128]{1,0:T(8,128)}, u32[]{:S(2)}) copy-start(f32[16,128]{1,0:T(8,128)} %get-tuple-element.5) | copy-start | bytes 24580

commit v4 on v3

--- a/solution.py
+++ b/solution.py
@@ -31,9 +31,9 @@
     load_send, load_land, load_own, load_all,
     inner_send, inner_land, inner_own, inner_all,
     adj_send, adj_land, adj_own, adj_all,
-    rhs_send, rhs_land, rhs_own, rhs_all,
+    rhs_send, rhs_land, rhs_far, rhs_relay, rhs_own, rhs_all,
     minner_send, minner_land, minner_own, minner_all,
-    madj_send, madj_land,
+    madj_send, madj_land, madj_far, madj_relay,
     send_sem, recv_sem,
 ):
     ny, nz, nx = dims
@@ -123,6 +123,68 @@
             between()
         whole.wait_recv()
         value = landing[...]
+        return value.reshape(-1, value.shape[-1])
+
+    leg = nz // 4
+
+    def at(step):
+        return lax.rem(z + (step + nz), nz)
+
+    def hop(slot, step, source, landing):
+        pltpu.make_async_remote_copy(
+            src_ref=source,
+            dst_ref=landing,
+            send_sem=send_sem.at[slot],
+            recv_sem=recv_sem.at[slot],
+            device_id=(leaf_of(y, at(step), c), x),
+            device_id_type=pl.DeviceIdType.MESH,
+        ).start()
+
+    def hop_waiter(slot, landing):
+        whole = pltpu.make_async_remote_copy(
+            src_ref=landing,
+            dst_ref=landing,
+            send_sem=send_sem.at[slot],
+            recv_sem=recv_sem.at[slot],
+            device_id=(leaf_of(y, at(1), c), x),
+            device_id_type=pl.DeviceIdType.MESH,
+        )
+        pending.append(whole)
+        return whole
+
+    def ring_sum(far_slot, slot, buffer, land, far, relay):
+        for step in range(leg, 0, -1):
+            hop(far_slot, step, buffer.at[at(step + leg)], far.at[step - 1])
+            if step < leg:
+                hop(far_slot, -step, buffer.at[at(-step - leg)], far.at[leg + step - 1])
+        for step in range(1, leg):
+            hop(slot, step, buffer.at[at(step)], land.at[2 * step - 2])
+            hop(slot, -step, buffer.at[at(-step)], land.at[2 * step - 1])
+        hop_waiter(far_slot, far).wait_recv()
+        relay[0] = buffer[at(leg)] + jnp.sum(far[:leg], axis=0)
+        hop(slot, leg, relay.at[0], land.at[2 * leg - 2])
+        back = buffer[at(-leg)]
+        relay[1] = back + jnp.sum(far[leg:], axis=0) if leg > 1 else back
+        hop(slot, -leg, relay.at[1], land.at[2 * leg - 1])
+        near_sum = buffer[z]
+        hop_waiter(slot, land).wait_recv()
+        return near_sum + jnp.sum(land[...], axis=0)
+
+    def ring_gather(far_slot, slot, own, land):
+        for step in (leg, -leg):
+            hop(far_slot, step, own, land.at[z])
+        for step in range(leg - 1, 0, -1):
+            hop(slot, step, own, land.at[z])
+            hop(slot, -step, own, land.at[z])
+        land[z] = own[...]
+        hop_waiter(far_slot, land.at[pl.ds(0, 2)]).wait_recv()
+        behind, ahead = at(-leg), at(leg)
+        for step in range(leg, 0, -1):
+            hop(slot, step, land.at[behind], land.at[behind])
+            if step < leg:
+                hop(slot, -step, land.at[ahead], land.at[ahead])
+        hop_waiter(slot, land.at[pl.ds(0, 4 * leg - 3)]).wait_recv()
+        value = land[...]
         return value.reshape(-1, value.shape[-1])
 
     barrier = pltpu.get_barrier_semaphore()
@@ -268,19 +330,19 @@
     mid_y_wait.wait_recv()
     mid_load = jnp.sum(mid_y_land[...], axis=0)
     rhs_send[...] = (mid_load - dot_split(couple, top_block)).reshape(rhs_send.shape)
-    rhs_own[...] = scatter_sum(13, "z", rhs_send, rhs_land)
+    rhs_own[...] = ring_sum(13, 19, rhs_send, rhs_land, rhs_far, rhs_relay)
     mid_wait.wait_recv()
     mid_t = mid_land[...].reshape(nz * mid_rows, width)
     mid_w = mid_t.T.astype(BF16)
     mid_t = mid_t.astype(BF16)
-    mid_rhs = gather(14, "z", rhs_own, rhs_all)
+    mid_rhs = ring_gather(14, 20, rhs_own, rhs_all)
 
     minner_send[...] = dot_split(mid_w, mid_rhs).reshape(minner_send.shape)
     minner_own[...] = scatter_sum(15, "half", minner_send, minner_land)
     mid_inner = gather(16, "half", minner_own, minner_all)
 
     madj_send[...] = dot_split(mid_t, mid_inner).reshape(madj_send.shape)
-    mid_out[...] = scatter_sum(17, "z", madj_send, madj_land)
+    mid_out[...] = ring_sum(17, 21, madj_send, madj_land, madj_far, madj_relay)
 
     for whole in pending:
         whole.wait_send()
@@ -305,6 +367,10 @@
 
     def reduce_gather(count, height):
         return exchange(count, height) + [buf(height, loads), buf(count, height, loads)]
+
+    def two_legs(height):
+        leg = nz // 4
+        return [buf(count, height, loads) for count in (nz, 2 * leg, 2 * leg - 1, 2)]
 
     plane = ny * nq
     scratch = (
@@ -320,10 +386,11 @@
         + reduce_gather(plane, z_width // plane)
         + [buf(nz, top_rows, loads)] * 2
         + [buf(top_rows, loads), buf(plane, top_rows, loads)]
-        + reduce_gather(nz, mid_rows)
+        + two_legs(mid_rows)
+        + [buf(mid_rows, loads), buf(nz, mid_rows, loads)]
         + reduce_gather(half * nq, z_width // (half * nq))
-        + exchange(nz, mid_rows)
-        + [pltpu.SemaphoreType.DMA((19,)), pltpu.SemaphoreType.DMA((19,))]
+        + two_legs(mid_rows)
+        + [pltpu.SemaphoreType.DMA((22,)), pltpu.SemaphoreType.DMA((22,))]
     )
     vmem = pl.BlockSpec(memory_space=pltpu.VMEM)
     return pl.pallas_call(

time: 110 us -> 112 us (1.018)
  Pallas kernels: 106 us -> 108 us
    pallas_call x1, Pallas kernels: 106 us -> 108 us  [body(): pl.pallas_call(functools.partial(kernel, dims), out_shape=(jax.ShapeDtype...]
where the time goes in v4:
time: 112 us; the launch traced here: 111 us
  Pallas kernels  108 us (96%)
  local copies, waits for them, and re-layouts  1.88 us (2%)
    pallas_call x1, Pallas kernels, body(): pl.pallas_call(functools.partial(kernel, dims), out_shape=(jax.ShapeDtype...  108 us

profile of v4, /device:TPU:1, one launch (start us, length us, event | category | flops | bytes accessed | tf_op | source)
XLA Modules:
  0.0 110.9 jit_solution(2148918585737917719)
XLA Ops:
  0.6 108.4 %adjoint.1 = (f32[8,128]{1,0:T(8,128)}, f32[16,128]{1,0:T(8,128)}) custom-call(bf16[32,8192]{1,0:T(8,128)(2,1)} %bitcast.4, bf16[32,128]{1,0:T(8,128)(2,1)} %bitcast.7, bf16[8,4096]{1,0:T(8,128)(2,1)} %bitcast.6, bf16[16,4096]{1,0:T(8,128)(2,1)} %bitcast.5, bf16[16,4096]{1,0:T(8,128)(2,1)} %coupling.1), custom_call_target="tpu_custom_call" | custom-call | tf_op jit(solution)/shard_map/adjoint/pallas_call | solution.py:396
  109.1 0.0 copy-start
  109.1 1.3 %copy.9 = f32[8,128]{1,0:T(8,128)} copy(f32[8,128]{1,0:T(8,128)} %get-tuple-element.4) | data formatting | bytes 8192
  110.3 0.0 copy-done
  110.3 0.6 copy.10
Async XLA Ops:
  109.1 1.3 %copy-start = (f32[16,128]{1,0:T(8,128)S(1)}, f32[16,128]{1,0:T(8,128)}, u32[]{:S(2)}) copy-start(f32[16,128]{1,0:T(8,128)} %get-tuple-element.5) | copy-start | bytes 24580

commit v5 on v3

--- a/solution.py
+++ b/solution.py
@@ -34,6 +34,7 @@
     rhs_send, rhs_land, rhs_own, rhs_all,
     minner_send, minner_land, minner_own, minner_all,
     madj_send, madj_land,
+    top_w, top_t, couple_blocks, mid_load, mid_w, mid_t,
     send_sem, recv_sem,
 ):
     ny, nz, nx = dims
@@ -240,46 +241,50 @@
 
     def factors_late():
         push(4, "z", columns(mid_send), mid_land, late)
+        couple_wait.wait_recv()
+        couple_blocks[...] = couple_land[...].reshape(nz * mid_rows, width).astype(BF16)
+        mid_y_wait.wait_recv()
+        mid_load[...] = jnp.sum(mid_y_land[...], axis=0)
+
+    def mid_ready():
+        mid_wait.wait_recv()
+        blocks = mid_land[...].reshape(nz * mid_rows, width)
+        mid_w[...] = blocks.T.astype(BF16)
+        mid_t[...] = blocks.astype(BF16)
 
     mid_wait = waiter(4, "z", mid_land)
 
     top_wait.wait_recv()
-    top_t = top_land[...].reshape(nz * top_rows, width)
-    top_w = top_t.T.astype(BF16)
-    top_t = top_t.astype(BF16)
+    blocks = top_land[...].reshape(nz * top_rows, width)
+    top_w[...] = blocks.T.astype(BF16)
+    top_t[...] = blocks.astype(BF16)
 
     top_y_wait.wait_recv()
     load_send[...] = jnp.sum(top_y_land[...], axis=0).reshape(load_send.shape)
     load_own[...] = scatter_sum(7, "z", load_send, load_land)
     top_load = gather(8, "z", load_own, load_all, mid_loads)
 
-    inner_send[...] = dot_split(top_w, top_load).reshape(inner_send.shape)
+    inner_send[...] = dot_split(top_w[...], top_load).reshape(inner_send.shape)
     inner_own[...] = scatter_sum(9, "plane", inner_send, inner_land, factors_early)
     top_inner = gather(10, "plane", inner_own, inner_all)
 
-    adj_send[...] = dot_split(top_t, top_inner).reshape(adj_send.shape)
+    adj_send[...] = dot_split(top_t[...], top_inner).reshape(adj_send.shape)
     adjoint = scatter_sum(11, "z", adj_send, adj_land)
     adj_own[...] = adjoint
     top_out[...] = adjoint
     top_block = gather(12, "plane", adj_own, adj_all, factors_late)
 
-    couple_wait.wait_recv()
-    couple = couple_land[...].reshape(nz * mid_rows, width).astype(BF16)
-    mid_y_wait.wait_recv()
-    mid_load = jnp.sum(mid_y_land[...], axis=0)
-    rhs_send[...] = (mid_load - dot_split(couple, top_block)).reshape(rhs_send.shape)
-    rhs_own[...] = scatter_sum(13, "z", rhs_send, rhs_land)
-    mid_wait.wait_recv()
-    mid_t = mid_land[...].reshape(nz * mid_rows, width)
-    mid_w = mid_t.T.astype(BF16)
-    mid_t = mid_t.astype(BF16)
+    rhs_send[...] = (mid_load[...] - dot_split(couple_blocks[...], top_block)).reshape(
+        rhs_send.shape
+    )
+    rhs_own[...] = scatter_sum(13, "z", rhs_send, rhs_land, mid_ready)
     mid_rhs = gather(14, "z", rhs_own, rhs_all)
 
-    minner_send[...] = dot_split(mid_w, mid_rhs).reshape(minner_send.shape)
+    minner_send[...] = dot_split(mid_w[...], mid_rhs).reshape(minner_send.shape)
     minner_own[...] = scatter_sum(15, "half", minner_send, minner_land)
     mid_inner = gather(16, "half", minner_own, minner_all)
 
-    madj_send[...] = dot_split(mid_t, mid_inner).reshape(madj_send.shape)
+    madj_send[...] = dot_split(mid_t[...], mid_inner).reshape(madj_send.shape)
     mid_out[...] = scatter_sum(17, "z", madj_send, madj_land)
 
     for whole in pending:
@@ -299,6 +304,9 @@
 
     def buf(*shape):
         return pltpu.VMEM(shape, F32)
+
+    def half_buf(*shape):
+        return pltpu.VMEM(shape, BF16)
 
     def exchange(count, height):
         return [buf(count, height, loads), buf(count, height, loads)]
@@ -323,6 +331,9 @@
         + reduce_gather(nz, mid_rows)
         + reduce_gather(half * nq, z_width // (half * nq))
         + exchange(nz, mid_rows)
+        + [half_buf(z_width, nz * top_rows), half_buf(nz * top_rows, z_width)]
+        + [half_buf(nz * mid_rows, z_width), buf(nz * mid_rows, loads)]
+        + [half_buf(z_width, nz * mid_rows), half_buf(nz * mid_rows, z_width)]
         + [pltpu.SemaphoreType.DMA((19,)), pltpu.SemaphoreType.DMA((19,))]
     )
     vmem = pl.BlockSpec(memory_space=pltpu.VMEM)

time: 110 us -> 110 us (level)
  no operation moved by 1% of the time
where the time goes in v5:
time: 110 us; the launch traced here: 109 us
  Pallas kernels  107 us (97%)
  local copies, waits for them, and re-layouts  1.88 us (2%)
    pallas_call x1, Pallas kernels, body(): pl.pallas_call(functools.partial(kernel, dims), out_shape=(jax.ShapeDtype...  107 us

profile of v5, /device:TPU:1, one launch (start us, length us, event | category | flops | bytes accessed | tf_op | source)
XLA Modules:
  0.0 109.1 jit_solution(16766623905572858000)
XLA Ops:
  0.6 106.5 %adjoint.1 = (f32[8,128]{1,0:T(8,128)}, f32[16,128]{1,0:T(8,128)}) custom-call(bf16[32,8192]{1,0:T(8,128)(2,1)} %bitcast.4, bf16[32,128]{1,0:T(8,128)(2,1)} %bitcast.7, bf16[8,4096]{1,0:T(8,128)(2,1)} %bitcast.6, bf16[16,4096]{1,0:T(8,128)(2,1)} %bitcast.5, bf16[16,4096]{1,0:T(8,128)(2,1)} %coupling.1), custom_call_target="tpu_custom_call" | custom-call | tf_op jit(solution)/shard_map/adjoint/pallas_call | solution.py:340
  107.2 0.0 copy-start
  107.2 1.3 %copy.9 = f32[8,128]{1,0:T(8,128)} copy(f32[8,128]{1,0:T(8,128)} %get-tuple-element.4) | data formatting | bytes 8192
  108.5 0.0 copy-done
  108.5 0.6 copy.10
Async XLA Ops:
  107.2 1.3 %copy-start = (f32[16,128]{1,0:T(8,128)S(1)}, f32[16,128]{1,0:T(8,128)}, u32[]{:S(2)}) copy-start(f32[16,128]{1,0:T(8,128)} %get-tuple-element.5) | copy-start | bytes 24580

commit v6 on v5

--- a/solution.py
+++ b/solution.py
@@ -161,7 +161,6 @@
     sol_wait = send(0, "q", lambda peer: sol_send, sol_land)
     border_wait = send(1, "q", lambda peer: border_send.at[0, peer], border_land.at[0])
     near = groups["z"][2][::-1]
-    early, late = near[: 2 * len(near) // 3], near[2 * len(near) // 3 :]
     push(2, "z", columns(top_send), top_land, near)
     top_wait = waiter(2, "z", top_land)
     regroup(1, mid_rows)
@@ -189,7 +188,7 @@
             )
 
     couple_rows = lambda peer: couple_send.at[peer]
-    push(3, "z", couple_rows, couple_land, early)
+    push(3, "z", couple_rows, couple_land, near)
     couple_wait = waiter(3, "z", couple_land)
     couple_land[z] = couple_send[z]
     mid_send[...] = mid_factor[...].astype(F32)
@@ -235,12 +234,10 @@
 
     mid_y_wait = waiter(6, "pair", mid_y_land)
 
-    def factors_early():
-        push(3, "z", couple_rows, couple_land, late)
-        push(4, "z", columns(mid_send), mid_land, early)
-
-    def factors_late():
-        push(4, "z", columns(mid_send), mid_land, late)
+    def send_mid_factor():
+        push(4, "z", columns(mid_send), mid_land, near)
+
+    def couple_ready():
         couple_wait.wait_recv()
         couple_blocks[...] = couple_land[...].reshape(nz * mid_rows, width).astype(BF16)
         mid_y_wait.wait_recv()
@@ -265,14 +262,14 @@
     top_load = gather(8, "z", load_own, load_all, mid_loads)
 
     inner_send[...] = dot_split(top_w[...], top_load).reshape(inner_send.shape)
-    inner_own[...] = scatter_sum(9, "plane", inner_send, inner_land, factors_early)
+    inner_own[...] = scatter_sum(9, "plane", inner_send, inner_land, send_mid_factor)
     top_inner = gather(10, "plane", inner_own, inner_all)
 
     adj_send[...] = dot_split(top_t[...], top_inner).reshape(adj_send.shape)
     adjoint = scatter_sum(11, "z", adj_send, adj_land)
     adj_own[...] = adjoint
     top_out[...] = adjoint
-    top_block = gather(12, "plane", adj_own, adj_all, factors_late)
+    top_block = gather(12, "plane", adj_own, adj_all, couple_ready)
 
     rhs_send[...] = (mid_load[...] - dot_split(couple_blocks[...], top_block)).reshape(
         rhs_send.shape

time: 110 us -> 110 us (level); the launches traced: 109 us -> 110 us
    pallas_call x1, Pallas kernels: 107 us -> 108 us  [body(): pl.pallas_call(functools.partial(kernel, dims), out_shape=(jax.ShapeDtype...]
where the time goes in v6:
time: 110 us
  Pallas kernels  108 us (98%)
  local copies, waits for them, and re-layouts  1.88 us (2%)
    pallas_call x1, Pallas kernels, body(): pl.pallas_call(functools.partial(kernel, dims), out_shape=(jax.ShapeDtype...  108 us

profile of v6, /device:TPU:1, one launch (start us, length us, event | category | flops | bytes accessed | tf_op | source)
XLA Modules:
  0.0 110.2 jit_solution(8501366771742217195)
XLA Ops:
  0.6 107.7 %adjoint.1 = (f32[8,128]{1,0:T(8,128)}, f32[16,128]{1,0:T(8,128)}) custom-call(bf16[32,8192]{1,0:T(8,128)(2,1)} %bitcast.4, bf16[32,128]{1,0:T(8,128)(2,1)} %bitcast.7, bf16[8,4096]{1,0:T(8,128)(2,1)} %bitcast.6, bf16[16,4096]{1,0:T(8,128)(2,1)} %bitcast.5, bf16[16,4096]{1,0:T(8,128)(2,1)} %coupling.1), custom_call_target="tpu_custom_call" | custom-call | tf_op jit(solution)/shard_map/adjoint/pallas_call | solution.py:337
  108.3 0.0 copy-start
  108.3 1.3 %copy.9 = f32[8,128]{1,0:T(8,128)} copy(f32[8,128]{1,0:T(8,128)} %get-tuple-element.4) | data formatting | bytes 8192
  109.6 0.0 copy-done
  109.6 0.6 copy.10
Async XLA Ops:
  108.3 1.3 %copy-start = (f32[16,128]{1,0:T(8,128)S(1)}, f32[16,128]{1,0:T(8,128)}, u32[]{:S(2)}) copy-start(f32[16,128]{1,0:T(8,128)} %get-tuple-element.5) | copy-start | bytes 24580

commit v7 on v6

--- a/solution.py
+++ b/solution.py
@@ -16,9 +16,9 @@
 def dot_split(factor, value):
     high = value.astype(BF16)
     low = (value - high.astype(F32)).astype(BF16)
-    return jnp.dot(factor, low, preferred_element_type=F32) + jnp.dot(
-        factor, high, preferred_element_type=F32
-    )
+    both = jnp.dot(factor, jnp.concatenate([low, high], 1), preferred_element_type=F32)
+    count = value.shape[1]
+    return both[:, :count] + both[:, count:]
 
 
 def kernel(

time: 110 us -> 110 us (level)
  no operation moved by 1% of the time
where the time goes in v7:
time: 110 us
  Pallas kernels  107 us (97%)
  local copies, waits for them, and re-layouts  1.88 us (2%)
    pallas_call x1, Pallas kernels, body(): pl.pallas_call(functools.partial(kernel, dims), out_shape=(jax.ShapeDtype...  107 us

profile of v7, /device:TPU:1, one launch (start us, length us, event | category | flops | bytes accessed | tf_op | source)
XLA Modules:
  0.0 109.9 jit_solution(906507767782950828)
XLA Ops:
  0.6 107.4 %adjoint.1 = (f32[8,128]{1,0:T(8,128)}, f32[16,128]{1,0:T(8,128)}) custom-call(bf16[32,8192]{1,0:T(8,128)(2,1)} %bitcast.4, bf16[32,128]{1,0:T(8,128)(2,1)} %bitcast.7, bf16[8,4096]{1,0:T(8,128)(2,1)} %bitcast.6, bf16[16,4096]{1,0:T(8,128)(2,1)} %bitcast.5, bf16[16,4096]{1,0:T(8,128)(2,1)} %coupling.1), custom_call_target="tpu_custom_call" | custom-call | tf_op jit(solution)/shard_map/adjoint/pallas_call | solution.py:337
  108.0 0.0 copy-start
  108.0 1.3 %copy.9 = f32[8,128]{1,0:T(8,128)} copy(f32[8,128]{1,0:T(8,128)} %get-tuple-element.4) | data formatting | bytes 8192
  109.3 0.0 copy-done
  109.3 0.6 copy.10
Async XLA Ops:
  108.0 1.3 %copy-start = (f32[16,128]{1,0:T(8,128)S(1)}, f32[16,128]{1,0:T(8,128)}, u32[]{:S(2)}) copy-start(f32[16,128]{1,0:T(8,128)} %get-tuple-element.5) | copy-start | bytes 24580
